TPU v7x, 512 devices: a whole 4x8x8 slice. The times are simulated.
512 devices in a mesh: row: 16 (over x_hi, y), col: 32 (over z, x_lo, core).
Axes of the slice: x: 4 (x_hi: 2, x_lo: 2; x = x_hi * 2 + x_lo), y: 8, z: 8, core: 2. Of those that a mesh axis runs over, the one named last changes fastest.
Arguments:
- base_input: bfloat16 [1024, 16384], P('col', 'row'), may hold values from -6 to 6
- layer_input: bfloat16 [1024, 16384], P('row', 'col'), may hold values from -6 to 6
- out_grad: bfloat16 [1024, 16384], P('col', 'row'), may hold values from -6 to 6
- cross_weight: bfloat16 [16384, 16384], P('row', 'col'), may hold values from -0.046875 to 0.046875
- cross_bias: bfloat16 [16384], P('row'), may hold values from -5 to 5
Outputs:
- weight_grad: float32 [16384, 16384], P('row', 'col')
- bias_grad: float32 [16384], P('row')
- base_grad: bfloat16 [1024, 16384], P('col', 'row')
- branch_grad: bfloat16 [1024, 16384], P('row', 'col')
All inputs are finite; a program needn't handle non-finite values.
Results may differ from a plain program's by a relative error of at most 0.019.
Values may be sent and summed in bfloat16 or wider, within the bound.
A program may use at most 64 MiB of HBM per device.

v0:
```python
import jax
import jax.numpy as jnp
from jax import lax
from jax.sharding import PartitionSpec as P


def on_device(base_input, layer_input, out_grad, cross_weight, cross_bias):
    input_panel = lax.all_gather(layer_input, "row", axis=0, tiled=True)
    grad_panel, base_panel = (
        lax.all_gather(out_grad, "col", axis=0, tiled=True),
        lax.all_gather(base_input, "col", axis=0, tiled=True),
    )
    hidden_panel = (grad_panel.astype(jnp.float32) * base_panel.astype(jnp.float32)).astype(
        jnp.bfloat16
    )
    weight_grad = lax.dot_general(
        hidden_panel, input_panel, (((0,), (0,)), ((), ())), preferred_element_type=jnp.float32
    )
    bias_grad = jnp.sum(hidden_panel, axis=0, dtype=jnp.float32)
    rows = input_panel
    preact = lax.psum_scatter(
        lax.dot_general(
            rows, cross_weight, (((1,), (1,)), ((), ())), preferred_element_type=jnp.float32
        ).astype(jnp.bfloat16),
        "col",
        scatter_dimension=0,
        tiled=True,
    ).astype(jnp.float32)
    preact = preact + cross_bias.astype(jnp.float32)[None, :]
    base_grad = (out_grad.astype(jnp.float32) * preact).astype(jnp.bfloat16)
    rows = hidden_panel
    branch = lax.psum_scatter(
        jnp.dot(rows, cross_weight, preferred_element_type=jnp.float32).astype(jnp.bfloat16),
        "row",
        scatter_dimension=0,
        tiled=True,
    )
    return (weight_grad, bias_grad, base_grad, branch)


def solution(mesh):
    in_specs = (P("col", "row"), P("row", "col"), P("col", "row"), P("row", "col"), P("row"))
    out_specs = (P("row", "col"), P("row"), P("col", "row"), P("row", "col"))
    return jax.shard_map(
        on_device, mesh=mesh, in_specs=in_specs, out_specs=out_specs, check_vma=False
    )
```

profile of v0, /device:TPU:16, one launch (start us, length us, event | category | flops | bytes accessed | tf_op | source)
XLA Modules:
  0.0 573.2 jit_solution(8535226228451038034)
XLA Ops:
  7.2 0.0 copy-start
  7.2 0.0 all-gather.8.cloned.1.call-start
  7.2 0.7 all-gather.8.cloned.1.call-update
  7.9 0.0 all-gather.6.cloned.1.call-start
  8.0 0.7 all-gather.6.cloned.1.call-update
  8.7 0.0 all-gather.4.cloned.1.call-start
  8.7 0.7 all-gather.4.cloned.1.call-update
  9.4 0.0 reduce-scatter.3.cloned.1.call-start
  9.4 89.4 %all-gather.8.cloned.1.call-done = bf16[1024,512]{1,0:T(8,128)(2,1)} async-done(((bf16[64,512]{1,0:T(8,128)(2,1)}), bf16[1024,512]{1,0:T(8,128)(2,1)}) %all-gather.8.cloned.1.call-update) | async-done | bytes 1048592 | tf_op jit(solution)/shard_map/all_gather | solution.py:8
  98.9 0.0 copy-done
  98.9 3.8 convolution_convert_fusion
  102.7 0.0 reduce-scatter.3.cloned.1.call-update
  102.7 0.0 copy-start.4
  102.7 0.0 reduce-scatter.5.cloned.1.call-start
  102.8 63.9 %all-gather.6.cloned.1.call-done = bf16[1024,1024]{1,0:T(8,128)(2,1)} async-done(((bf16[32,1024]{1,0:T(8,128)(2,1)}), bf16[1024,1024]{1,0:T(8,128)(2,1)}) %all-gather.6.cloned.1.call-update) | async-done | bytes 2097168 | tf_op jit(solution)/shard_map/all_gather | solution.py:11
  166.7 69.4 %all-gather.4.cloned.1.call-done = bf16[1024,1024]{1,0:T(8,128)(2,1)} async-done(((bf16[32,1024]{1,0:T(8,128)(2,1)}), bf16[1024,1024]{1,0:T(8,128)(2,1)}) %all-gather.4.cloned.1.call-update) | async-done | bytes 2097168 | tf_op jit(solution)/shard_map/all_gather | solution.py:10
  236.0 0.0 copy-start.1
  236.0 4.6 convolution_convert_fusion.1
  240.7 0.0 reduce-scatter.5.cloned.1.call-update
  240.7 0.0 copy-done.4
  240.7 0.0 copy-done.1
  240.7 0.0 copy-start.2
  240.7 0.0 copy-start.5
  240.8 3.3 convert_reduce_fusion
  244.1 0.0 copy-done.2
  244.1 0.0 copy-done.5
  244.1 0.0 copy-start.3
  244.1 2.6 fusion
  246.7 113.2 %reduce-scatter.3.cloned.1.call-done = bf16[32,1024]{1,0:T(8,128)(2,1)} async-done(((bf16[1024,1024]{1,0:T(8,128)(2,1)}), bf16[32,1024]{1,0:T(8,128)(2,1)}) %reduce-scatter.3.cloned.1.call-update) | async-done | bytes 65552 | tf_op jit(solution)/shard_map/reduce_scatter | solution.py:21
  359.9 0.0 copy-done.3
  359.9 1.5 multiply_convert_fusion.1
  361.4 205.3 %reduce-scatter.5.cloned.1.call-done = bf16[64,512]{1,0:T(8,128)(2,1)} async-done(((bf16[1024,512]{1,0:T(8,128)(2,1)}), bf16[64,512]{1,0:T(8,128)(2,1)}) %reduce-scatter.5.cloned.1.call-update) | async-done | bytes 65552 | tf_op jit(solution)/shard_map/reduce_scatter | solution.py:32
  (1 shorter events, 0.0 us)
Async XLA Ops:
  7.2 91.7 %copy-start = (bf16[1024,512]{1,0:T(8,128)(2,1)S(1)}, bf16[1024,512]{1,0:T(8,128)(2,1)}, u32[]{:S(2)}) copy-start(bf16[1024,512]{1,0:T(8,128)(2,1)} %param.8) | copy-start | bytes 3145732
  7.2 91.7 %all-gather.8.cloned.1.call-start = ((), (), s32[]{:S(2)}) async-start(), calls=%async_computation.4 | async-start | bytes 1114112 | tf_op jit(solution)/shard_map/all_gather | solution.py:8
  7.9 158.7 %all-gather.6.cloned.1.call-start = ((), (), s32[]{:S(2)}) async-start(), calls=%async_computation.3 | async-start | bytes 2162688 | tf_op jit(solution)/shard_map/all_gather | solution.py:11
  8.7 227.4 %all-gather.4.cloned.1.call-start = ((), (), s32[]{:S(2)}) async-start(), calls=%async_computation.2 | async-start | bytes 2162688 | tf_op jit(solution)/shard_map/all_gather | solution.py:10
  9.4 350.5 %reduce-scatter.3.cloned.1.call-start = ((), (), s32[]{:S(2)}) async-start(), calls=%async_computation.5 | async-start | bytes 2162688 | tf_op jit(solution)/shard_map/reduce_scatter | solution.py:21
  102.7 138.0 %copy-start.4 = (bf16[1024]{0:T(1024)(128)(2,1)S(1)}, bf16[1024]{0:T(1024)(128)(2,1)}, u32[]{:S(2)}) copy-start(bf16[1024]{0:T(1024)(128)(2,1)} %param.9) | copy-start | bytes 6148
  102.7 463.9 %reduce-scatter.5.cloned.1.call-start = ((), (), s32[]{:S(2)}) async-start(), calls=%async_computation.6 | async-start | bytes 1114112 | tf_op jit(solution)/shard_map/reduce_scatter | solution.py:32
  236.0 4.7 copy-start.1
  240.7 3.3 copy-start.2
  240.7 3.3 copy-start.5
  244.1 115.8 %copy-start.3 = (bf16[32,1024]{1,0:T(8,128)(2,1)S(1)}, bf16[32,1024]{1,0:T(8,128)(2,1)}, u32[]{:S(2)}) copy-start(bf16[32,1024]{1,0:T(8,128)(2,1)} %param.7) | copy-start | bytes 196612
Sparse Core Ops, SparseCore 0:
  11.2 87.6 all-gather.7
  101.0 65.6 all-gather.5
  168.8 67.1 all-gather.3
  238.7 121.1 reduce-scatter.2
  365.4 201.2 reduce-scatter.4
where the time goes:
time: 573 us
  waiting for transfers between devices  543 us (95%)
  between operations  13.8 us (2%)
  matrix products  11.1 us (2%)
    reduce_scatter x1, waiting for transfers between devices, on_device(): lax.psum_scatter(jnp.dot(rows, cross_weight, preferred_element_type=jnp.f...  205 us
    reduce_scatter x1, waiting for transfers between devices, on_device(): lax.psum_scatter(lax.dot_general(rows, cross_weight, (((1,), (1,)), ((),...  113 us
    all_gather x1, waiting for transfers between devices, on_device(): input_panel = lax.all_gather(layer_input, 'row', axis=0, tiled=True)  89.4 us
    all_gather x1, waiting for transfers between devices, on_device(): lax.all_gather(out_grad, 'col', axis=0, tiled=True)  69.4 us
    all_gather x1, waiting for transfers between devices, on_device(): lax.all_gather(base_input, 'col', axis=0, tiled=True)  63.9 us
  transfers between devices with their start and end apart: 5, of which 5 were waited for; matrix products, arithmetic and copies ran while one was open for 3% of the time, Pallas kernels for 0%

commit v1 on v0

--- a/solution.py
+++ b/solution.py
@@ -8,7 +8,9 @@
     input_panel = lax.all_gather(layer_input, "row", axis=0, tiled=True)
     grad_panel, base_panel = (
         lax.all_gather(out_grad, "col", axis=0, tiled=True),
-        lax.all_gather(base_input, "col", axis=0, tiled=True),
+        jnp.concatenate(
+            lax.all_to_all(jnp.stack([base_input] * lax.axis_size("col")), "col", 0, 0), axis=0
+        ),
     )
     hidden_panel = (grad_panel.astype(jnp.float32) * base_panel.astype(jnp.float32)).astype(
         jnp.bfloat16

time: 573 us -> 505 us (0.88)
  waiting for transfers between devices: 543 us -> 460 us
  starting transfers between devices: 0.19 us -> 11.8 us
    all_gather x1 -> x0, waiting for transfers between devices: 63.9 us -> none  [on_device(): lax.all_gather(base_input, 'col', axis=0, tiled=True)]
    all_gather x1, waiting for transfers between devices: 89.4 us -> 76.3 us  [on_device(): input_panel = lax.all_gather(layer_input, 'row', axis=0, tiled=True)]
    all_to_all x0 -> x1, starting transfers between devices: none -> 11.6 us  [on_device(): lax.all_to_all(jnp.stack([base_input] * lax.axis_size('col')), 'col', 0, 0)]
  transfers between devices with their start and end apart: 5 -> 5, of which waited for: 5 -> 4; matrix products, arithmetic and copies ran while one was open for 3% -> 3% of each run, Pallas kernels for 0% -> 0%
where the time goes in v1:
time: 505 us; the launch traced here: 504 us
  waiting for transfers between devices  460 us (91%)
  between operations  13.8 us (3%)
  starting transfers between devices  11.8 us (2%)
  matrix products  10.3 us (2%)
    reduce_scatter x1, waiting for transfers between devices, on_device(): lax.psum_scatter(jnp.dot(rows, cross_weight, preferred_element_type=jnp.f...  205 us
    reduce_scatter x1, waiting for transfers between devices, on_device(): lax.psum_scatter(lax.dot_general(rows, cross_weight, (((1,), (1,)), ((),...  113 us
    all_gather x1, waiting for transfers between devices, on_device(): input_panel = lax.all_gather(layer_input, 'row', axis=0, tiled=True)  76.3 us
    all_gather x1, waiting for transfers between devices, on_device(): lax.all_gather(out_grad, 'col', axis=0, tiled=True)  63.9 us
    all_to_all x1, starting transfers between devices, on_device(): lax.all_to_all(jnp.stack([base_input] * lax.axis_size('col')), 'col', 0, 0)  11.6 us
  transfers between devices with their start and end apart: 5, of which 4 were waited for; matrix products, arithmetic and copies ran while one was open for 3% of the time, Pallas kernels for 0%

profile of v1, /device:TPU:16, one launch (start us, length us, event | category | flops | bytes accessed | tf_op | source)
XLA Modules:
  0.0 504.3 jit_solution(2644778537750879070)
XLA Ops:
  7.2 0.0 copy-start
  7.2 0.0 all-gather.5.cloned.1.call-start
  7.2 0.7 all-gather.5.cloned.1.call-update
  7.9 0.0 all-gather.3.cloned.1.call-start
  8.0 0.7 all-gather.3.cloned.1.call-update
  8.7 2.4 stack.2
  11.1 11.6 %all-to-all-start = ((bf16[32,32,1024]{2,1,0:T(8,128)(2,1)}), bf16[32,32,1024]{2,1,0:T(8,128)(2,1)S(1)}, u32[]{:S(2)}, u32[]{:S(2)}) async-start(bf16[32,32,1024]{2,1,0:T(8,128)(2,1)} %stack.2), calls=%async_computation | async-start | bytes 4194304 | tf_op jit(solution)/shard_map/all_to_all | solution.py:12
  22.7 0.0 reduce-scatter.3.cloned.1.call-start
  22.8 76.3 %all-gather.5.cloned.1.call-done = bf16[1024,512]{1,0:T(8,128)(2,1)} async-done(((bf16[64,512]{1,0:T(8,128)(2,1)}), bf16[1024,512]{1,0:T(8,128)(2,1)}) %all-gather.5.cloned.1.call-update) | async-done | bytes 1048592 | tf_op jit(solution)/shard_map/all_gather | solution.py:8
  99.1 0.0 copy-done
  99.1 3.8 convolution_convert_fusion
  102.9 0.0 reduce-scatter.3.cloned.1.call-update
  103.0 0.0 reduce-scatter.5.cloned.1.call-start
  103.0 0.0 all-to-all-done
  103.0 63.9 %all-gather.3.cloned.1.call-done = bf16[1024,1024]{1,0:T(8,128)(2,1)} async-done(((bf16[32,1024]{1,0:T(8,128)(2,1)}), bf16[1024,1024]{1,0:T(8,128)(2,1)}) %all-gather.3.cloned.1.call-update) | async-done | bytes 2097168 | tf_op jit(solution)/shard_map/all_gather | solution.py:10
  166.9 3.4 convert_reduce_fusion
  170.3 0.0 copy-start.1
  170.3 1.3 copy-done.1
  171.6 0.0 copy-start.3
  171.6 0.0 copy-start.4
  171.6 2.2 convolution_convert_fusion.1
  173.8 0.0 reduce-scatter.5.cloned.1.call-update
  173.8 0.0 copy-done.3
  173.9 0.0 copy-done.4
  173.9 0.0 copy-start.2
  173.9 4.2 fusion.2
  178.1 112.8 %reduce-scatter.3.cloned.1.call-done = bf16[32,1024]{1,0:T(8,128)(2,1)} async-done(((bf16[1024,1024]{1,0:T(8,128)(2,1)}), bf16[32,1024]{1,0:T(8,128)(2,1)}) %reduce-scatter.3.cloned.1.call-update) | async-done | bytes 65552 | tf_op jit(solution)/shard_map/reduce_scatter | solution.py:23
  290.9 0.0 copy-done.2
  290.9 1.5 multiply_convert_fusion
  292.4 205.3 %reduce-scatter.5.cloned.1.call-done = bf16[64,512]{1,0:T(8,128)(2,1)} async-done(((bf16[1024,512]{1,0:T(8,128)(2,1)}), bf16[64,512]{1,0:T(8,128)(2,1)}) %reduce-scatter.5.cloned.1.call-update) | async-done | bytes 65552 | tf_op jit(solution)/shard_map/reduce_scatter | solution.py:34
  (1 shorter events, 0.0 us)
Async XLA Ops:
  7.2 91.9 %copy-start = (bf16[1024,512]{1,0:T(8,128)(2,1)S(1)}, bf16[1024,512]{1,0:T(8,128)(2,1)}, u32[]{:S(2)}) copy-start(bf16[1024,512]{1,0:T(8,128)(2,1)} %param.8) | copy-start | bytes 3145732
  7.2 91.9 %all-gather.5.cloned.1.call-start = ((), (), s32[]{:S(2)}) async-start(), calls=%async_computation.4 | async-start | bytes 1114112 | tf_op jit(solution)/shard_map/all_gather | solution.py:8
  7.9 159.0 %all-gather.3.cloned.1.call-start = ((), (), s32[]{:S(2)}) async-start(), calls=%async_computation.3 | async-start | bytes 2162688 | tf_op jit(solution)/shard_map/all_gather | solution.py:10
  11.1 91.9 %all-to-all-start = ((bf16[32,32,1024]{2,1,0:T(8,128)(2,1)}), bf16[32,32,1024]{2,1,0:T(8,128)(2,1)S(1)}, u32[]{:S(2)}, u32[]{:S(2)}) async-start(bf16[32,32,1024]{2,1,0:T(8,128)(2,1)} %stack.2), calls=%async_computation | async-start | bytes 4194304 | tf_op jit(solution)/shard_map/all_to_all | solution.py:12
  22.7 268.2 %reduce-scatter.3.cloned.1.call-start = ((), (), s32[]{:S(2)}) async-start(), calls=%async_computation.5 | async-start | bytes 2162688 | tf_op jit(solution)/shard_map/reduce_scatter | solution.py:23
  103.0 394.8 %reduce-scatter.5.cloned.1.call-start = ((), (), s32[]{:S(2)}) async-start(), calls=%async_computation.6 | async-start | bytes 1114112 | tf_op jit(solution)/shard_map/reduce_scatter | solution.py:34
  170.3 1.3 copy-start.1
  171.6 2.3 copy-start.3
  171.6 2.3 copy-start.4
  173.9 117.0 %copy-start.2 = (bf16[32,1024]{1,0:T(8,128)(2,1)S(1)}, bf16[32,1024]{1,0:T(8,128)(2,1)}, u32[]{:S(2)}) copy-start(bf16[32,1024]{1,0:T(8,128)(2,1)} %param.7) | copy-start | bytes 196612
Sparse Core Ops, SparseCore 0:
  11.2 87.8 all-gather.4
  101.3 65.6 all-gather.2
  169.7 121.1 reduce-scatter.2
  296.4 201.3 reduce-scatter.4
